TPU v7x, 256 devices: a whole 4x4x8 slice. The times are simulated.
256 devices in a mesh: freq: 64 (over y, z, x_hi), inp: 4 (over x_lo, core).
Axes of the slice: x: 4 (x_hi: 2, x_lo: 2; x = x_hi * 2 + x_lo), y: 4, z: 8, core: 2. Of those that a mesh axis runs over, the one named last changes fastest.
Arguments:
- voltages: int32 [192, 2048, 1024], P('freq', None, 'inp'), may hold values from -128 to 127
- taps: float32 [12, 2048], replicated, may hold values from -0.013671875 to 0.013671875
- start: int32 [8, 2, 1024], replicated, may hold values from -127 to 127
Outputs:
- cleaned: bfloat16 [1024, 192, 2, 1024], P('freq', None, None, 'inp')
- ritz_matrix: float32 [1024, 8, 8], P('freq')
Inputs may be any that keep to these rules, and one draw needn't show every extreme that they name: `voltages`: 8-bit voltage samples.
All inputs are finite; a program needn't handle non-finite values.
Results may differ from a plain program's by a relative error of at most 0.0052.
Values may be sent and summed in bfloat16 or wider, within the bound.
No kernel may reach another device: no remote copies, remote signals or barrier semaphores. Data moves between devices by JAX's collectives and lax.ppermute only.
A program may use at most 192 MiB of HBM per device.

v0:
```python
import math
import jax
import jax.numpy as jnp
from jax import lax
from jax.sharding import PartitionSpec as P

ITERS = 4


def from_behind(value, axis, steps):
    count = lax.axis_size(axis)
    pairs = [(source, (source + steps) % count) for source in range(count)]
    return lax.ppermute(value, axis, pairs)


def project_rows(basis_rows, channel_data):
    projected = jnp.einsum(
        "ckr,cmr->ckm", basis_rows, channel_data, precision=lax.Precision.HIGHEST
    )
    return lax.psum(projected, "inp")


def subspace_clean(turned, start_block):
    highest = lax.Precision.HIGHEST
    channel_local, spectra_count, part_count, inputs_width = turned.shape
    row_count = part_count * inputs_width
    channel_data = turned.reshape(channel_local, spectra_count, row_count).astype(jnp.float32)
    start_rows = start_block.reshape(start_block.shape[0], row_count).astype(jnp.float32)
    basis_rows = jnp.broadcast_to(start_rows[None], (channel_local,) + start_rows.shape)
    for iteration in range(ITERS):
        projected = project_rows(basis_rows, channel_data)
        mapped = (
            jnp.einsum("ckm,cmr->ckr", projected, channel_data, precision=highest) / spectra_count
        )
        gram_matrix = jnp.einsum("ckr,cjr->ckj", mapped, mapped, precision=highest)
        gram_matrix = lax.psum(gram_matrix, "inp")
        lower_factor = jnp.linalg.cholesky(gram_matrix)
        basis_rows = lax.linalg.triangular_solve(lower_factor, mapped, left_side=True, lower=True)
    projected = project_rows(basis_rows, channel_data)
    ritz_matrix = (
        jnp.einsum("ckm,cjm->ckj", projected, projected, precision=highest) / spectra_count
    )
    cleaned = channel_data - jnp.einsum("ckm,ckr->cmr", projected, basis_rows, precision=highest)
    cleaned = cleaned.reshape(channel_local, spectra_count, part_count, inputs_width).astype(
        jnp.bfloat16
    )
    return (cleaned, ritz_matrix)


def shards(voltages, taps, start):
    slot_count = voltages.shape[0]
    frame_len = voltages.shape[1]
    inputs_local = voltages.shape[2]
    channel_count = frame_len // 2
    tap_count = taps.shape[0]
    frame_stack = voltages.astype(jnp.bfloat16)
    history_len = tap_count - 1
    group_count = lax.axis_size("freq")
    portions = [frame_stack]
    shift_count = (history_len - 1) // slot_count + 1
    for distance in range(1, shift_count + 1):
        first_frame = max(0, distance * slot_count - history_len)
        portion = frame_stack[first_frame:]
        offset_mod = distance % group_count
        arrived = from_behind(portion, "freq", offset_mod)
        portions = [arrived] + portions
    extended = jnp.concatenate(portions, axis=0)
    filtered = jnp.zeros((slot_count, frame_len, inputs_local), jnp.float32)
    for tap_index in range(tap_count):
        window = extended[tap_index : tap_index + slot_count].astype(jnp.float32)
        filtered = filtered + taps[tap_index][None, :, None] * window
    channel_idx = lax.broadcasted_iota(jnp.int32, (channel_count, frame_len), 0)
    sample_idx = lax.broadcasted_iota(jnp.int32, (channel_count, frame_len), 1)
    angles = (channel_idx * sample_idx % frame_len).astype(jnp.float32) * (
        2.0 * math.pi / frame_len
    )
    dft_scale = 1.0 / math.sqrt(channel_count)
    cosine = jnp.cos(angles)
    sine_table = jnp.sin(angles)
    real_part = (
        jnp.einsum("kn,sni->ksi", cosine, filtered, precision=lax.Precision.HIGHEST) * dft_scale
    )
    imag_part = (
        -jnp.einsum("kn,sni->ksi", sine_table, filtered, precision=lax.Precision.HIGHEST)
        * dft_scale
    )
    spectra = jnp.stack([real_part, imag_part], axis=2).astype(jnp.bfloat16)
    turned = lax.all_to_all(spectra, "freq", split_axis=0, concat_axis=1, tiled=True)
    start_local = lax.dynamic_slice_in_dim(
        start, lax.axis_index("inp") * inputs_local, inputs_local, 2
    )
    cleaned, ritz_matrix = subspace_clean(turned, start_local)
    return (cleaned, ritz_matrix)


def solution(mesh):
    placed = (P("freq", None, "inp"), P(), P())
    return jax.shard_map(
        shards,
        mesh=mesh,
        in_specs=placed,
        out_specs=(P("freq", None, None, "inp"), P("freq", None, None)),
        check_vma=False,
    )
```

profile of v0, /device:TPU:1, one launch (start us, length us, event | category | flops | bytes accessed | tf_op | source)
XLA Modules:
  0.0 1002.1 jit_solution(7785082553652282310)
XLA Ops:
  10.5 5.0 collective-permute-start.1
  18.9 3.4 collective-permute-start
  22.3 181.6 %collective-permute-done = bf16[2,2048,256]{2,1,0:T(8,128)(2,1)S(1)} collective-permute-done((bf16[2,2048,256]{2,1,0:T(8,128)(2,1)S(1)}, bf16[2,2048,256]{2,1,0:T(8,128)(2,1)S(1)}, u32[]{:S(2)}, u32[]{:S(2)}) %collective-permute-start) | collective-permute-done | bytes 2097184 | tf_op jit(solution)/shard_map/ppermute | solution.py:13
  204.6 16.6 %collective-permute-done.2 = bf16[3,2048,256]{2,1,0:T(8,128)(2,1)S(1)} collective-permute-done((bf16[3,2048,256]{2,1,0:T(8,128)(2,1)S(1)}, bf16[3,2048,256]{2,1,0:T(8,128)(2,1)S(1)}, u32[]{:S(2)}, u32[]{:S(2)}) %collective-permute-start.2) | collective-permute-done | bytes 3145760 | tf_op jit(solution)/shard_map/ppermute | solution.py:13
  221.6 70.7 %collective-permute-done.3 = bf16[3,2048,256]{2,1,0:T(8,128)(2,1)S(1)} collective-permute-done((bf16[3,2048,256]{2,1,0:T(8,128)(2,1)S(1)}, bf16[3,2048,256]{2,1,0:T(8,128)(2,1)S(1)}, u32[]{:S(2)}, u32[]{:S(2)}) %collective-permute-start.3) | collective-permute-done | bytes 3145760 | tf_op jit(solution)/shard_map/ppermute | solution.py:13
  292.5 9.7 multiply_add_fusion
  302.2 64.8 %fusion.19 = bf16[1024,3,1,256]{3,0,1,2:T(8,128)(2,1)S(1)} fusion(f32[3,2048,256]{2,1,0:T(8,128)} %multiply_add_fusion), kind=kOutput, calls=%fused_computation.25 | convolution fusion | flops 19358285824 | bytes 7864320 | tf_op jit(solution)/shard_map/kn,sni->ksi/dot_general | solution.py:81
  367.0 53.0 %fusion.22 = bf16[1024,3,1,256]{3,0,1,2:T(8,128)(2,1)S(1)} fusion(f32[3,2048,256]{2,1,0:T(8,128)S(1)} %copy-done), kind=kOutput, calls=%fused_computation.26 | convolution fusion | flops 19359072256 | bytes 7864320 | tf_op jit(solution)/shard_map/kn,sni->ksi/dot_general | solution.py:84
  420.3 4.9 copy.77
  425.2 98.1 %all-to-all-start = ((bf16[1024,3,2,256]{3,2,1,0:T(2,128)(2,1)}), bf16[1024,3,2,256]{3,2,1,0:T(2,128)(2,1)S(1)}, u32[]{:S(2)}, u32[]{:S(2)}) async-start(bf16[1024,3,2,256]{3,2,1,0:T(2,128)(2,1)} %copy.77), calls=%async_computation | async-start | bytes 6291456 | tf_op jit(solution)/shard_map/all_to_all | solution.py:88
  524.1 71.6 %all-to-all-done = bf16[1024,3,2,256]{3,2,1,0:T(2,128)(2,1)S(1)} async-done(((bf16[1024,3,2,256]{3,2,1,0:T(2,128)(2,1)}), bf16[1024,3,2,256]{3,2,1,0:T(2,128)(2,1)S(1)}, u32[]{:S(2)}, u32[]{:S(2)}) %all-to-all-start) | async-done | bytes 3145760 | tf_op jit(solution)/shard_map/all_to_all | solution.py:88
  595.7 4.7 copy.110
  600.4 4.6 reshape.41
  608.3 38.9 %all-reduce.6.cloned.1.call-done = f32[16,8,192]{2,1,0:T(8,128)} async-done(((f32[16,8,192]{2,1,0:T(8,128)}), f32[16,8,192]{2,1,0:T(8,128)}) %all-reduce.6.cloned.1.call-update) | async-done | bytes 98320 | tf_op jit(solution)/shard_map/psum | solution.py:20
  650.1 10.6 %psum.64 = f32[16,8,8]{1,2,0:T(8,128)S(1)} all-reduce(f32[16,8,8]{1,2,0:T(8,128)S(1)} %fusion.48), channel_id=1, replica_groups=mesh['freq'=64,'inp'=4] {'inp'}, use_global_device_ids=true, to_apply=%region_1.2 | all-reduce | flops 1024 | bytes 8192 | tf_op jit(solution)/shard_map/psum | solution.py:36
  661.4 12.4 %custom-call.12 = f32[16,8,8]{2,1,0:T(8,128)S(1)} custom-call(f32[16,8,8]{2,1,0:T(8,128)} %fusion.38), custom_call_target="Cholesky" | custom-call | tf_op jit(solution)/shard_map/jit(cholesky)/cholesky | solution.py:37
  674.1 10.0 custom-call.13
  688.3 42.2 %all-reduce.8.cloned.1.call-done = f32[16,8,192]{2,1,0:T(8,128)} async-done(((f32[16,8,192]{2,1,0:T(8,128)}), f32[16,8,192]{2,1,0:T(8,128)}) %all-reduce.8.cloned.1.call-update) | async-done | bytes 98320 | tf_op jit(solution)/shard_map/psum | solution.py:20
  733.3 10.6 %psum.66 = f32[16,8,8]{1,2,0:T(8,128)S(1)} all-reduce(f32[16,8,8]{1,2,0:T(8,128)S(1)} %fusion.50), channel_id=1, replica_groups=mesh['freq'=64,'inp'=4] {'inp'}, use_global_device_ids=true, to_apply=%region_5.8 | all-reduce | flops 1024 | bytes 8192 | tf_op jit(solution)/shard_map/psum | solution.py:36
  744.7 12.4 %custom-call.14 = f32[16,8,8]{2,1,0:T(8,128)S(1)} custom-call(f32[16,8,8]{2,1,0:T(8,128)} %fusion.35), custom_call_target="Cholesky" | custom-call | tf_op jit(solution)/shard_map/jit(cholesky)/cholesky | solution.py:37
  757.3 10.0 custom-call.15
  771.1 42.6 %all-reduce.10.cloned.1.call-done = f32[16,8,192]{2,1,0:T(8,128)} async-done(((f32[16,8,192]{2,1,0:T(8,128)}), f32[16,8,192]{2,1,0:T(8,128)}) %all-reduce.10.cloned.1.call-update) | async-done | bytes 98320 | tf_op jit(solution)/shard_map/psum | solution.py:20
  816.6 10.6 %psum.68 = f32[16,8,8]{1,2,0:T(8,128)S(1)} all-reduce(f32[16,8,8]{1,2,0:T(8,128)S(1)} %fusion.52), channel_id=1, replica_groups=mesh['freq'=64,'inp'=4] {'inp'}, use_global_device_ids=true, to_apply=%region_7.10 | all-reduce | flops 1024 | bytes 8192 | tf_op jit(solution)/shard_map/psum | solution.py:36
  827.9 12.4 %custom-call.16 = f32[16,8,8]{2,1,0:T(8,128)S(1)} custom-call(f32[16,8,8]{2,1,0:T(8,128)} %fusion.32), custom_call_target="Cholesky" | custom-call | tf_op jit(solution)/shard_map/jit(cholesky)/cholesky | solution.py:37
  840.6 10.0 custom-call.17
  854.4 42.6 %all-reduce.12.cloned.1.call-done = f32[16,8,192]{2,1,0:T(8,128)} async-done(((f32[16,8,192]{2,1,0:T(8,128)}), f32[16,8,192]{2,1,0:T(8,128)}) %all-reduce.12.cloned.1.call-update) | async-done | bytes 98320 | tf_op jit(solution)/shard_map/psum | solution.py:20
  899.9 10.8 %psum.70 = f32[16,8,8]{1,2,0:T(8,128)S(1)} all-reduce(f32[16,8,8]{1,2,0:T(8,128)S(1)} %fusion.54), channel_id=1, replica_groups=mesh['freq'=64,'inp'=4] {'inp'}, use_global_device_ids=true, to_apply=%region_9.12 | all-reduce | flops 1024 | bytes 8192 | tf_op jit(solution)/shard_map/psum | solution.py:36
  911.4 12.4 %custom-call.18 = f32[16,8,8]{2,1,0:T(8,128)S(1)} custom-call(f32[16,8,8]{2,1,0:T(8,128)} %fusion.29), custom_call_target="Cholesky" | custom-call | tf_op jit(solution)/shard_map/jit(cholesky)/cholesky | solution.py:37
  924.0 10.0 custom-call.19
  938.5 42.7 %all-reduce.14.cloned.1.call-done = f32[16,8,192]{2,1,0:T(8,128)} async-done(((f32[16,8,192]{2,1,0:T(8,128)}), f32[16,8,192]{2,1,0:T(8,128)}) %all-reduce.14.cloned.1.call-update) | async-done | bytes 98320 | tf_op jit(solution)/shard_map/psum | solution.py:20
  981.2 7.7 subtract_convert_fusion
  988.9 5.5 convert_element_type.82
  (76 shorter events, 44.5 us)
Async XLA Ops:
  7.2 15.1 %copy-start.3 = (f32[12,2048]{1,0:T(8,128)S(1)}, f32[12,2048]{1,0:T(8,128)}, u32[]{:S(2)}) copy-start(f32[12,2048]{1,0:T(8,128)} %param.7) | copy-start | bytes 294916
  10.5 193.6 %collective-permute-start.1 = (bf16[3,2048,256]{2,1,0:T(8,128)(2,1)S(1)}, bf16[3,2048,256]{2,1,0:T(8,128)(2,1)S(1)}, u32[]{:S(2)}, u32[]{:S(2)}) collective-permute-start(bf16[3,2048,256]{2,1,0:T(8,128)(2,1)S(1)} %convert_element_type.65), channel_id=1, source_target_pairs={{0,12},{4,16},{8,20},{12,24},{16,28},{20,32},{24,36},{28,40},{32,4... | collective-permute-start | bytes 9437192 | tf_op jit(solution)/shard_map/ppermute | solution.py:13
  15.5 205.7 %collective-permute-start.2 = (bf16[3,2048,256]{2,1,0:T(8,128)(2,1)S(1)}, bf16[3,2048,256]{2,1,0:T(8,128)(2,1)S(1)}, u32[]{:S(2)}, u32[]{:S(2)}) collective-permute-start(bf16[3,2048,256]{2,1,0:T(8,128)(2,1)S(1)} %convert_element_type.65), channel_id=1, source_target_pairs={{0,8},{4,12},{8,16},{12,20},{16,24},{20,28},{24,32},{28,36},{32,40... | collective-permute-start | bytes 9437192 | tf_op jit(solution)/shard_map/ppermute | solution.py:13
  17.2 275.1 %collective-permute-start.3 = (bf16[3,2048,256]{2,1,0:T(8,128)(2,1)S(1)}, bf16[3,2048,256]{2,1,0:T(8,128)(2,1)S(1)}, u32[]{:S(2)}, u32[]{:S(2)}) collective-permute-start(bf16[3,2048,256]{2,1,0:T(8,128)(2,1)S(1)} %convert_element_type.65), channel_id=1, source_target_pairs={{0,4},{4,8},{8,12},{12,16},{16,20},{20,24},{24,28},{28,32},{32,36}... | collective-permute-start | bytes 9437192 | tf_op jit(solution)/shard_map/ppermute | solution.py:13
  18.9 185.1 %collective-permute-start = (bf16[2,2048,256]{2,1,0:T(8,128)(2,1)S(1)}, bf16[2,2048,256]{2,1,0:T(8,128)(2,1)S(1)}, u32[]{:S(2)}, u32[]{:S(2)}) collective-permute-start(bf16[2,2048,256]{2,1,0:T(8,128)(2,1)S(1)} %slice.98), channel_id=1, source_target_pairs={{0,16},{4,20},{8,24},{12,28},{16,32},{20,36},{24,40},{28,44},{32,4... | collective-permute-start | bytes 6291464 | tf_op jit(solution)/shard_map/ppermute | solution.py:13
  302.2 64.8 %copy-start = (f32[3,2048,256]{2,1,0:T(8,128)S(1)}, f32[3,2048,256]{2,1,0:T(8,128)}, u32[]{:S(2)}) copy-start(f32[3,2048,256]{2,1,0:T(8,128)} %multiply_add_fusion) | copy-start | bytes 18874372
  425.2 170.6 %all-to-all-start = ((bf16[1024,3,2,256]{3,2,1,0:T(2,128)(2,1)}), bf16[1024,3,2,256]{3,2,1,0:T(2,128)(2,1)S(1)}, u32[]{:S(2)}, u32[]{:S(2)}) async-start(bf16[1024,3,2,256]{3,2,1,0:T(2,128)(2,1)} %copy.77), calls=%async_computation | async-start | bytes 6291456 | tf_op jit(solution)/shard_map/all_to_all | solution.py:88
  523.3 123.9 %all-reduce.6.cloned.1.call-start = ((), (), s32[]{:S(2)}) async-start(), calls=%async_computation.1 | async-start | bytes 262144 | tf_op jit(solution)/shard_map/psum | solution.py:20
  608.2 122.3 %all-reduce.8.cloned.1.call-start = ((), (), s32[]{:S(2)}) async-start(), calls=%async_computation.2 | async-start | bytes 262144 | tf_op jit(solution)/shard_map/psum | solution.py:20
  687.8 126.0 %all-reduce.10.cloned.1.call-start = ((), (), s32[]{:S(2)}) async-start(), calls=%async_computation.3 | async-start | bytes 262144 | tf_op jit(solution)/shard_map/psum | solution.py:20
  771.1 126.0 %all-reduce.12.cloned.1.call-start = ((), (), s32[]{:S(2)}) async-start(), calls=%async_computation.4 | async-start | bytes 262144 | tf_op jit(solution)/shard_map/psum | solution.py:20
  854.3 126.8 %all-reduce.14.cloned.1.call-start = ((), (), s32[]{:S(2)}) async-start(), calls=%async_computation.5 | async-start | bytes 262144 | tf_op jit(solution)/shard_map/psum | solution.py:20
  934.6 0.7 copy-start.1
  981.2 13.2 %copy-start.2 = (f32[16,8,192]{2,1,0:T(8,128)S(1)}, f32[16,8,192]{2,1,0:T(8,128)}, u32[]{:S(2)}) copy-start(f32[16,8,192]{2,1,0:T(8,128)} %all-reduce.14.cloned.1.call-done) | copy-start | bytes 294916
Sparse Core Ops, SparseCore 0:
  608.4 38.8 all-reduce.5
  687.9 42.5 all-reduce.7
  771.2 42.5 all-reduce.9
  854.4 42.5 all-reduce.11
  938.6 42.5 all-reduce.13
where the time goes:
time: 1010 us; the launch traced here: 1000 us
  waiting for transfers between devices  550 us (54%)
  matrix products  155 us (15%)
  starting transfers between devices  110 us (11%)
  other arithmetic  107 us (11%)
  blocking collectives  42.7 us (4%)
  local copies, waits for them, and re-layouts  23 us (2%)
  between operations  14.2 us (1%)
    ppermute x4, waiting for transfers between devices, from_behind(): return lax.ppermute(value, axis, pairs)  269 us
    psum x5, waiting for transfers between devices, project_rows(): return lax.psum(projected, 'inp')  209 us
    all_to_all x1, starting transfers between devices, shards(): lax.all_to_all(spectra, 'freq', split_axis=0, concat_axis=1, tiled=True)  98.1 us
    all_to_all x1, waiting for transfers between devices, shards(): lax.all_to_all(spectra, 'freq', split_axis=0, concat_axis=1, tiled=True)  71.6 us
    dot_general x1, matrix products, shards(): jnp.einsum('kn,sni->ksi', cosine, filtered, precision=lax.Precision.HIGHEST)  64.8 us
    dot_general x1, matrix products, shards(): jnp.einsum('kn,sni->ksi', sine_table, filtered, precision=lax.Precision.H...  53 us
    another operation x13, other arithmetic, subspace_clean(): lower_factor = jnp.linalg.cholesky(gram_matrix)  49.9 us
    psum x4, blocking collectives, subspace_clean(): gram_matrix = lax.psum(gram_matrix, 'inp')  42.7 us
  transfers between devices with their start and end apart: 10, of which 9 were waited for; matrix products, arithmetic and copies ran while one was open for 0% of the time, Pallas kernels for 0%

commit v1 on v0

--- a/solution.py
+++ b/solution.py
@@ -85,7 +85,10 @@
         * dft_scale
     )
     spectra = jnp.stack([real_part, imag_part], axis=2).astype(jnp.bfloat16)
-    turned = lax.all_to_all(spectra, "freq", split_axis=0, concat_axis=1, tiled=True)
+    turned = jnp.concatenate(
+        lax.all_to_all(jnp.stack(jnp.split(spectra, lax.axis_size("freq"), axis=0)), "freq", 0, 0),
+        axis=1,
+    )
     start_local = lax.dynamic_slice_in_dim(
         start, lax.axis_index("inp") * inputs_local, inputs_local, 2
     )

time: 1010 us -> 1040 us (1.030)
  other arithmetic: 107 us -> 147 us
    unnamed x1 -> x64, other arithmetic: 0.73 us -> 40 us
where the time goes in v1:
time: 1040 us
  waiting for transfers between devices  550 us (53%)
  matrix products  155 us (15%)
  other arithmetic  147 us (14%)
  starting transfers between devices  110 us (11%)
  blocking collectives  42.8 us (4%)
  local copies, waits for them, and re-layouts  17.9 us (2%)
  between operations  14.5 us (1%)
    ppermute x4, waiting for transfers between devices, from_behind(): return lax.ppermute(value, axis, pairs)  269 us
    psum x5, waiting for transfers between devices, project_rows(): return lax.psum(projected, 'inp')  210 us
    all_to_all x1, starting transfers between devices, shards(): lax.all_to_all(jnp.stack(jnp.split(spectra, lax.axis_size('freq'), axis=0...  98.1 us
    all_to_all x1, waiting for transfers between devices, shards(): lax.all_to_all(jnp.stack(jnp.split(spectra, lax.axis_size('freq'), axis=0...  71.6 us
    dot_general x1, matrix products, shards(): jnp.einsum('kn,sni->ksi', cosine, filtered, precision=lax.Precision.HIGHEST)  64.6 us
    dot_general x1, matrix products, shards(): jnp.einsum('kn,sni->ksi', sine_table, filtered, precision=lax.Precision.H...  52.9 us
    another operation x13, other arithmetic, subspace_clean(): lower_factor = jnp.linalg.cholesky(gram_matrix)  49.9 us
    psum x4, blocking collectives, subspace_clean(): gram_matrix = lax.psum(gram_matrix, 'inp')  42.8 us
  transfers between devices with their start and end apart: 10, of which 9 were waited for; matrix products, arithmetic and copies ran while one was open for 0% of the time, Pallas kernels for 0%

profile of v1, /device:TPU:1, one launch (start us, length us, event | category | flops | bytes accessed | tf_op | source)
XLA Modules:
  0.0 1036.7 jit_solution(8521765933143031136)
XLA Ops:
  7.2 3.3 convert_element_type.65
  10.5 5.0 collective-permute-start.1
  18.9 3.4 collective-permute-start
  22.3 181.6 %collective-permute-done = bf16[2,2048,256]{2,1,0:T(8,128)(2,1)S(1)} collective-permute-done((bf16[2,2048,256]{2,1,0:T(8,128)(2,1)S(1)}, bf16[2,2048,256]{2,1,0:T(8,128)(2,1)S(1)}, u32[]{:S(2)}, u32[]{:S(2)}) %collective-permute-start) | collective-permute-done | bytes 2097184 | tf_op jit(solution)/shard_map/ppermute | solution.py:13
  204.5 16.6 %collective-permute-done.2 = bf16[3,2048,256]{2,1,0:T(8,128)(2,1)S(1)} collective-permute-done((bf16[3,2048,256]{2,1,0:T(8,128)(2,1)S(1)}, bf16[3,2048,256]{2,1,0:T(8,128)(2,1)S(1)}, u32[]{:S(2)}, u32[]{:S(2)}) %collective-permute-start.2) | collective-permute-done | bytes 3145760 | tf_op jit(solution)/shard_map/ppermute | solution.py:13
  221.6 70.7 %collective-permute-done.3 = bf16[3,2048,256]{2,1,0:T(8,128)(2,1)S(1)} collective-permute-done((bf16[3,2048,256]{2,1,0:T(8,128)(2,1)S(1)}, bf16[3,2048,256]{2,1,0:T(8,128)(2,1)S(1)}, u32[]{:S(2)}, u32[]{:S(2)}) %collective-permute-start.3) | collective-permute-done | bytes 3145760 | tf_op jit(solution)/shard_map/ppermute | solution.py:13
  292.5 9.7 multiply_add_fusion
  302.2 64.6 %fusion.19 = bf16[1024,3,1,256]{3,0,1,2:T(8,128)(2,1)S(1)} fusion(f32[3,2048,256]{2,1,0:T(8,128)} %multiply_add_fusion), kind=kOutput, calls=%fused_computation.149 | convolution fusion | flops 19358285824 | bytes 7864320 | tf_op jit(solution)/shard_map/kn,sni->ksi/dot_general | solution.py:81
  366.8 52.9 %fusion.22 = bf16[1024,3,1,256]{3,0,1,2:T(8,128)(2,1)S(1)} fusion(f32[3,2048,256]{2,1,0:T(8,128)S(1)} %copy-done), kind=kOutput, calls=%fused_computation.150 | convolution fusion | flops 19359072256 | bytes 7864320 | tf_op jit(solution)/shard_map/kn,sni->ksi/dot_general | solution.py:84
  459.7 98.1 %all-to-all-start = ((bf16[64,16,3,2,256]{4,1,2,3,0:T(8,128)(2,1)}), bf16[64,16,3,2,256]{4,1,2,3,0:T(8,128)(2,1)S(1)}, u32[]{:S(2)}, u32[]{:S(2)}) async-start(bf16[64,16,3,2,256]{4,1,2,3,0:T(8,128)(2,1)} %constant_dynamic-update-slice_fusion.6), calls=%async_computation | async-start | bytes 6291456 | tf_op jit(solution)/shard_map/all_to_all | solution.py:89
  558.6 71.6 %all-to-all-done = bf16[64,16,3,2,256]{4,1,2,3,0:T(8,128)(2,1)S(1)} async-done(((bf16[64,16,3,2,256]{4,1,2,3,0:T(8,128)(2,1)}), bf16[64,16,3,2,256]{4,1,2,3,0:T(8,128)(2,1)S(1)}, u32[]{:S(2)}, u32[]{:S(2)}) %all-to-all-start) | async-done | bytes 3145760 | tf_op jit(solution)/shard_map/all_to_all | solution.py:89
  630.2 4.5 copy.58
  634.7 4.6 reshape_reshape.3
  642.6 38.9 %all-reduce.6.cloned.1.call-done = f32[16,8,192]{2,1,0:T(8,128)} async-done(((f32[16,8,192]{2,1,0:T(8,128)}), f32[16,8,192]{2,1,0:T(8,128)}) %all-reduce.6.cloned.1.call-update) | async-done | bytes 98320 | tf_op jit(solution)/shard_map/psum | solution.py:20
  684.4 10.6 %psum.64 = f32[16,8,8]{1,2,0:T(8,128)S(1)} all-reduce(f32[16,8,8]{1,2,0:T(8,128)S(1)} %fusion.112), channel_id=1, replica_groups=mesh['freq'=64,'inp'=4] {'inp'}, use_global_device_ids=true, to_apply=%region_1.2 | all-reduce | flops 1024 | bytes 8192 | tf_op jit(solution)/shard_map/psum | solution.py:36
  695.7 12.4 %custom-call.12 = f32[16,8,8]{2,1,0:T(8,128)S(1)} custom-call(f32[16,8,8]{2,1,0:T(8,128)} %fusion.38), custom_call_target="Cholesky" | custom-call | tf_op jit(solution)/shard_map/jit(cholesky)/cholesky | solution.py:37
  708.4 10.0 custom-call.13
  722.1 42.7 %all-reduce.8.cloned.1.call-done = f32[16,8,192]{2,1,0:T(8,128)} async-done(((f32[16,8,192]{2,1,0:T(8,128)}), f32[16,8,192]{2,1,0:T(8,128)}) %all-reduce.8.cloned.1.call-update) | async-done | bytes 98320 | tf_op jit(solution)/shard_map/psum | solution.py:20
  767.6 10.9 %psum.66 = f32[16,8,8]{1,2,0:T(8,128)S(1)} all-reduce(f32[16,8,8]{1,2,0:T(8,128)S(1)} %fusion.114), channel_id=1, replica_groups=mesh['freq'=64,'inp'=4] {'inp'}, use_global_device_ids=true, to_apply=%region_5.8 | all-reduce | flops 1024 | bytes 8192 | tf_op jit(solution)/shard_map/psum | solution.py:36
  779.2 12.4 %custom-call.14 = f32[16,8,8]{2,1,0:T(8,128)S(1)} custom-call(f32[16,8,8]{2,1,0:T(8,128)} %fusion.35), custom_call_target="Cholesky" | custom-call | tf_op jit(solution)/shard_map/jit(cholesky)/cholesky | solution.py:37
  791.9 10.0 custom-call.15
  805.7 42.6 %all-reduce.10.cloned.1.call-done = f32[16,8,192]{2,1,0:T(8,128)} async-done(((f32[16,8,192]{2,1,0:T(8,128)}), f32[16,8,192]{2,1,0:T(8,128)}) %all-reduce.10.cloned.1.call-update) | async-done | bytes 98320 | tf_op jit(solution)/shard_map/psum | solution.py:20
  851.1 10.6 %psum.68 = f32[16,8,8]{1,2,0:T(8,128)S(1)} all-reduce(f32[16,8,8]{1,2,0:T(8,128)S(1)} %fusion.116), channel_id=1, replica_groups=mesh['freq'=64,'inp'=4] {'inp'}, use_global_device_ids=true, to_apply=%region_7.10 | all-reduce | flops 1024 | bytes 8192 | tf_op jit(solution)/shard_map/psum | solution.py:36
  862.5 12.4 %custom-call.16 = f32[16,8,8]{2,1,0:T(8,128)S(1)} custom-call(f32[16,8,8]{2,1,0:T(8,128)} %fusion.32), custom_call_target="Cholesky" | custom-call | tf_op jit(solution)/shard_map/jit(cholesky)/cholesky | solution.py:37
  875.1 10.0 custom-call.17
  888.9 42.6 %all-reduce.12.cloned.1.call-done = f32[16,8,192]{2,1,0:T(8,128)} async-done(((f32[16,8,192]{2,1,0:T(8,128)}), f32[16,8,192]{2,1,0:T(8,128)}) %all-reduce.12.cloned.1.call-update) | async-done | bytes 98320 | tf_op jit(solution)/shard_map/psum | solution.py:20
  934.4 10.6 %psum.70 = f32[16,8,8]{1,2,0:T(8,128)S(1)} all-reduce(f32[16,8,8]{1,2,0:T(8,128)S(1)} %fusion.118), channel_id=1, replica_groups=mesh['freq'=64,'inp'=4] {'inp'}, use_global_device_ids=true, to_apply=%region_9.12 | all-reduce | flops 1024 | bytes 8192 | tf_op jit(solution)/shard_map/psum | solution.py:36
  945.8 12.4 %custom-call.18 = f32[16,8,8]{2,1,0:T(8,128)S(1)} custom-call(f32[16,8,8]{2,1,0:T(8,128)} %fusion.29), custom_call_target="Cholesky" | custom-call | tf_op jit(solution)/shard_map/jit(cholesky)/cholesky | solution.py:37
  958.4 10.0 custom-call.19
  972.8 42.7 %all-reduce.14.cloned.1.call-done = f32[16,8,192]{2,1,0:T(8,128)} async-done(((f32[16,8,192]{2,1,0:T(8,128)}), f32[16,8,192]{2,1,0:T(8,128)}) %all-reduce.14.cloned.1.call-update) | async-done | bytes 98320 | tf_op jit(solution)/shard_map/psum | solution.py:20
  1015.5 7.7 subtract_convert_fusion
  1023.3 5.5 convert_element_type.82
  (138 shorter events, 80.4 us)
Async XLA Ops:
  10.5 11.8 %copy-start.3 = (f32[12,2048]{1,0:T(8,128)S(1)}, f32[12,2048]{1,0:T(8,128)}, u32[]{:S(2)}) copy-start(f32[12,2048]{1,0:T(8,128)} %param.7) | copy-start | bytes 294916
  10.5 193.6 %collective-permute-start.1 = (bf16[3,2048,256]{2,1,0:T(8,128)(2,1)S(1)}, bf16[3,2048,256]{2,1,0:T(8,128)(2,1)S(1)}, u32[]{:S(2)}, u32[]{:S(2)}) collective-permute-start(bf16[3,2048,256]{2,1,0:T(8,128)(2,1)S(1)} %convert_element_type.65), channel_id=1, source_target_pairs={{0,12},{4,16},{8,20},{12,24},{16,28},{20,32},{24,36},{28,40},{32,4... | collective-permute-start | bytes 9437192 | tf_op jit(solution)/shard_map/ppermute | solution.py:13
  15.5 205.7 %collective-permute-start.2 = (bf16[3,2048,256]{2,1,0:T(8,128)(2,1)S(1)}, bf16[3,2048,256]{2,1,0:T(8,128)(2,1)S(1)}, u32[]{:S(2)}, u32[]{:S(2)}) collective-permute-start(bf16[3,2048,256]{2,1,0:T(8,128)(2,1)S(1)} %convert_element_type.65), channel_id=1, source_target_pairs={{0,8},{4,12},{8,16},{12,20},{16,24},{20,28},{24,32},{28,36},{32,40... | collective-permute-start | bytes 9437192 | tf_op jit(solution)/shard_map/ppermute | solution.py:13
  17.1 275.1 %collective-permute-start.3 = (bf16[3,2048,256]{2,1,0:T(8,128)(2,1)S(1)}, bf16[3,2048,256]{2,1,0:T(8,128)(2,1)S(1)}, u32[]{:S(2)}, u32[]{:S(2)}) collective-permute-start(bf16[3,2048,256]{2,1,0:T(8,128)(2,1)S(1)} %convert_element_type.65), channel_id=1, source_target_pairs={{0,4},{4,8},{8,12},{12,16},{16,20},{20,24},{24,28},{28,32},{32,36}... | collective-permute-start | bytes 9437192 | tf_op jit(solution)/shard_map/ppermute | solution.py:13
  18.9 185.1 %collective-permute-start = (bf16[2,2048,256]{2,1,0:T(8,128)(2,1)S(1)}, bf16[2,2048,256]{2,1,0:T(8,128)(2,1)S(1)}, u32[]{:S(2)}, u32[]{:S(2)}) collective-permute-start(bf16[2,2048,256]{2,1,0:T(8,128)(2,1)S(1)} %slice.98), channel_id=1, source_target_pairs={{0,16},{4,20},{8,24},{12,28},{16,32},{20,36},{24,40},{28,44},{32,4... | collective-permute-start | bytes 6291464 | tf_op jit(solution)/shard_map/ppermute | solution.py:13
  302.2 64.6 %copy-start = (f32[3,2048,256]{2,1,0:T(8,128)S(1)}, f32[3,2048,256]{2,1,0:T(8,128)}, u32[]{:S(2)}) copy-start(f32[3,2048,256]{2,1,0:T(8,128)} %multiply_add_fusion) | copy-start | bytes 18874372
  459.7 170.5 %all-to-all-start = ((bf16[64,16,3,2,256]{4,1,2,3,0:T(8,128)(2,1)}), bf16[64,16,3,2,256]{4,1,2,3,0:T(8,128)(2,1)S(1)}, u32[]{:S(2)}, u32[]{:S(2)}) async-start(bf16[64,16,3,2,256]{4,1,2,3,0:T(8,128)(2,1)} %constant_dynamic-update-slice_fusion.6), calls=%async_computation | async-start | bytes 6291456 | tf_op jit(solution)/shard_map/all_to_all | solution.py:89
  557.8 123.7 %all-reduce.6.cloned.1.call-start = ((), (), s32[]{:S(2)}) async-start(), calls=%async_computation.1 | async-start | bytes 262144 | tf_op jit(solution)/shard_map/psum | solution.py:20
  642.5 122.3 %all-reduce.8.cloned.1.call-start = ((), (), s32[]{:S(2)}) async-start(), calls=%async_computation.2 | async-start | bytes 262144 | tf_op jit(solution)/shard_map/psum | solution.py:20
  722.1 126.2 %all-reduce.10.cloned.1.call-start = ((), (), s32[]{:S(2)}) async-start(), calls=%async_computation.3 | async-start | bytes 262144 | tf_op jit(solution)/shard_map/psum | solution.py:20
  805.6 126.0 %all-reduce.12.cloned.1.call-start = ((), (), s32[]{:S(2)}) async-start(), calls=%async_computation.4 | async-start | bytes 262144 | tf_op jit(solution)/shard_map/psum | solution.py:20
  888.9 126.6 %all-reduce.14.cloned.1.call-start = ((), (), s32[]{:S(2)}) async-start(), calls=%async_computation.5 | async-start | bytes 262144 | tf_op jit(solution)/shard_map/psum | solution.py:20
  968.9 0.7 copy-start.1
  1023.2 5.5 copy-start.2
Sparse Core Ops, SparseCore 0:
  642.6 38.8 all-reduce.5
  722.2 42.5 all-reduce.7
  805.8 42.5 all-reduce.9
  889.0 42.5 all-reduce.11
  973.0 42.5 all-reduce.13
